TPU v7x, 32 devices: a whole 2x2x4 slice. The times are simulated.
32 devices in a mesh: dp: 8 (over z, core), seq: 4 (over y, x).
Axes of the slice: x: 2, y: 2, z: 4, core: 2. Of those that a mesh axis runs over, the one named last changes fastest.
Arguments:
- waveform: bfloat16 [32, 2560], P('dp', 'seq'), may hold values from -6 to 6
- lengths: int32 [8, 4], P('dp'), may hold values from 1 to 2560, 6400 in all within a row
- conv_one: bfloat16 [10, 512], replicated, may hold values from -2 to 2
- conv_two: bfloat16 [1536, 512], replicated, may hold values from -0.15625 to 0.15625
- gain_one: float32 [512], replicated, may hold values from 0.1 to 1.9
- shift_one: float32 [512], replicated, may hold values from -3 to 3
- gain_two: float32 [512], replicated, may hold values from 0.1 to 1.9
- shift_two: float32 [512], replicated, may hold values from -3 to 3
- cotangent: bfloat16 [32, 256, 512], P('dp', 'seq'), may hold values from -0.0625 to 0.0625
Outputs:
- features: bfloat16 [32, 256, 512], P('dp', 'seq')
- conv_one_grad: float32 [10, 512], replicated
- conv_two_grad: float32 [1536, 512], P('seq')
- norm_grads: float32 [4, 512], replicated
Inputs may be any that keep to these rules, and one draw needn't show every extreme that they name: In each row of lengths the 4 lengths sum to 6400 and the longest is exactly 2560.
All inputs are finite; a program needn't handle non-finite values.
Results may differ from a plain program's by a relative error of at most 0.0054.
Values may be sent and summed in bfloat16 or wider, within the bound.
A program may use at most 64 MiB of HBM per device.

v0:
```python
import jax
import jax.numpy as jnp
from jax import lax
from jax.sharding import PartitionSpec as P

epsilon = 1e-05
root_half = 0.7071067811865476
normal_peak = 0.3989422804014327


def passed_along(value, axis, steps):
    count = lax.axis_size(axis)
    first, last = (max(0, -steps), min(count, count - steps))
    return lax.ppermute(value, axis, [(source, source + steps) for source in range(first, last)])


def norm_forward(preact, gain_vector, offset):
    centre = preact - jnp.mean(preact, axis=-1, keepdims=True)
    inverse = lax.rsqrt(jnp.mean(centre * centre, axis=-1, keepdims=True) + epsilon)
    normed = centre * inverse
    return (normed, inverse, normed * gain_vector + offset)


def gelu_slope(values):
    return (
        0.5 * (1.0 + lax.erf(values * root_half))
        + values * jnp.exp(-0.5 * values * values) * normal_peak
    )


def norm_backward(upstream, normed, inverse, gain_vector):
    scaled = upstream * gain_vector
    return inverse * (
        scaled
        - jnp.mean(scaled, axis=-1, keepdims=True)
        - normed * jnp.mean(scaled * normed, axis=-1, keepdims=True)
    )


def on_device(
    waveform, lengths, conv_one, conv_two, gain_one, shift_one, gain_two, shift_two, cotangent
):
    clip_count, samples = waveform.shape
    frames_one = samples // 5
    frames_two = cotangent.shape[1]
    channels = conv_two.shape[1]
    position = lax.axis_index("seq")
    border = passed_along(waveform[:, :16], "seq", -1)
    extended = jnp.concatenate([waveform, border], axis=1)
    blocks = extended[:, : 5 * (frames_one + 1)].reshape(clip_count, frames_one + 1, 5)
    patch_one = jnp.concatenate([blocks[:, :-1], blocks[:, 1:]], axis=2).reshape(
        clip_count * frames_one, 10
    )
    pre_one = jnp.dot(patch_one, conv_one, preferred_element_type=jnp.float32)
    normed_one, inverse_one, output_one = norm_forward(pre_one, gain_one, shift_one)
    active_one = (
        jax.nn.gelu(output_one, approximate=False)
        .astype(jnp.bfloat16)
        .reshape(clip_count, frames_one, channels)
    )
    edge_frame = passed_along(active_one[:, :1], "seq", -1)
    widened = jnp.concatenate([active_one, edge_frame], axis=1)
    patch_two = jnp.concatenate(
        [widened[:, :frames_one].reshape(clip_count, frames_two, 2 * channels), widened[:, 2::2]],
        axis=2,
    ).reshape(clip_count * frames_two, 3 * channels)
    pre_two = jnp.dot(patch_two, conv_two, preferred_element_type=jnp.float32)
    normed_two, inverse_two, output_two = norm_forward(pre_two, gain_two, shift_two)
    lengths_row = lengths[0]
    first_frames = (lengths_row - 5) // 5
    second_frames = (first_frames - 1) // 2
    frame_index = position * frames_two + lax.broadcasted_iota(
        jnp.int32, (clip_count, frames_two), 1
    )
    validity = (
        (frame_index < second_frames[:, None])
        .astype(jnp.float32)
        .reshape(clip_count * frames_two, 1)
    )
    features = (
        (jax.nn.gelu(output_two, approximate=False) * validity)
        .astype(jnp.bfloat16)
        .reshape(clip_count, frames_two, channels)
    )
    upstream_two = (
        cotangent.reshape(clip_count * frames_two, channels).astype(jnp.float32)
        * validity
        * gelu_slope(output_two)
    )
    dpre_two = norm_backward(upstream_two, normed_two, inverse_two, gain_two).astype(jnp.bfloat16)
    dpatch_two = lax.dot_general(
        dpre_two, conv_two, (((1,), (1,)), ((), ())), preferred_element_type=jnp.float32
    ).reshape(clip_count, frames_two, 3 * channels)
    paired = dpatch_two[:, :, : 2 * channels].reshape(clip_count, frames_two, 2, channels)
    onward = dpatch_two[:, :, 2 * channels :]
    carried = jnp.concatenate([passed_along(onward[:, -1:], "seq", 1), onward[:, :-1]], axis=1)
    dact_one = jnp.stack([paired[:, :, 0] + carried, paired[:, :, 1]], axis=2).reshape(
        clip_count, frames_one, channels
    )
    upstream_one = dact_one.reshape(clip_count * frames_one, channels) * gelu_slope(output_one)
    dpre_one = norm_backward(upstream_one, normed_one, inverse_one, gain_one)
    grad_one = lax.dot_general(
        patch_one.astype(jnp.float32),
        dpre_one,
        (((0,), (0,)), ((), ())),
        precision=lax.Precision.HIGHEST,
        preferred_element_type=jnp.float32,
    )
    norm_terms = jnp.stack(
        [
            jnp.sum(upstream_one * normed_one, 0),
            jnp.sum(upstream_one, 0),
            jnp.sum(upstream_two * normed_two, 0),
            jnp.sum(upstream_two, 0),
        ]
    )
    grad_one_sum, norm_sum = lax.psum((grad_one, norm_terms), ("dp", "seq"))
    seq_share = lax.psum_scatter(
        lax.dot_general(
            patch_two, dpre_two, (((0,), (0,)), ((), ())), preferred_element_type=jnp.float32
        ),
        "seq",
        scatter_dimension=0,
        tiled=True,
    )
    grad_two = lax.psum(seq_share, "dp")
    return (features, grad_one_sum, grad_two, norm_sum)


def solution(mesh):
    in_specs = (P("dp", "seq"), P("dp", None), P(), P(), P(), P(), P(), P(), P("dp", "seq", None))
    out_specs = (P("dp", "seq", None), P(), P("seq", None), P())
    return jax.shard_map(
        on_device, mesh=mesh, in_specs=in_specs, out_specs=out_specs, check_vma=False
    )
```

profile of v0, /device:TPU:0, one launch (start us, length us, event | category | flops | bytes accessed | tf_op | source)
XLA Modules:
  0.0 152.2 jit_solution(17305733421126608220)
XLA Ops:
  8.0 1.3 collective-permute-start
  10.0 4.4 %collective-permute-done = bf16[4,16]{1,0:T(4,128)(2,1)S(1)} collective-permute-done((bf16[4,16]{1,0:T(4,128)(2,1)S(1)}, bf16[4,16]{1,0:T(4,128)(2,1)S(1)}, u32[]{:S(2)}, u32[]{:S(2)}) %collective-permute-start) | collective-permute-done | bytes 160 | tf_op jit(solution)/shard_map/ppermute | solution.py:14
  15.7 1.1 fusion.49
  17.1 3.0 %fusion.2 = bf16[512,512]{1,0:T(8,128)(2,1)S(1)} fusion(f32[512,512]{1,0:T(8,128)S(1)} %get-tuple-element.22, f32[512]{0:T(512)S(1)} %copy-done.6, f32[512]{0:T(512)S(1)} %copy-done.5, f32[512]{0:T(512)S(1)} %add_rsqrt_fusion, f32[512]{0:T(512)S(1)} %broadcast_multiply_fusion.2), kind=kLoop, calls=%fused_computation.4 | loop fusion | flops 18087936 | bytes 1581056 | tf_op jit(solution)/shard_map/convert_element_type | solution.py:58
  20.1 1.3 collective-permute-start.1
  21.6 1.0 concatenate.27
  22.6 4.0 %collective-permute-done.1 = bf16[4,1,512]{2,1,0:T(2,128)(2,1)S(1)} collective-permute-done((bf16[4,1,512]{2,1,0:T(2,128)(2,1)S(1)}, bf16[4,1,512]{2,1,0:T(2,128)(2,1)S(1)}, u32[]{:S(2)}, u32[]{:S(2)}) %collective-permute-start.1) | collective-permute-done | bytes 4128 | tf_op jit(solution)/shard_map/ppermute | solution.py:14
  27.4 2.1 %slice.41 = bf16[4,64,512]{2,1,0:T(8,128)(2,1)S(1)} slice(bf16[4,129,512]{2,1,0:T(8,128)(2,1)} %pad_maximum_fusion.2), slice={[0:4:1], [2:129:2], [0:512:1]} | slice | bytes 524288 | tf_op jit(solution)/shard_map/slice | solution.py:64
  29.6 1.7 %fusion.50 = (f32[256]{0:T(256)S(1)}, f32[256,512]{1,0:T(8,128)S(1)}) fusion(bf16[1536,512]{1,0:T(8,128)(2,1)S(1)} %copy-done, bf16[256,512]{1,0:T(8,128)(2,1)S(1)} %bitcast.39, bf16[256,1024]{1,0:T(8,128)(2,1)} %concatenate.27), kind=kOutput, calls=%fused_computation.105 | convolution fusion | flops 404356864 | bytes 2884608 | tf_op jit(solution)/shard_map/dot_general | solution.py:67
  31.6 2.5 %multiply_reduce_fusion.4 = (f32[512]{0:T(512)S(1)}, f32[256]{0:T(256)S(1)}, f32[256]{0:T(256)S(1)}, f32[512]{0:T(512)S(1)}, f32[256,512]{1,0:T(8,128)S(1)}, /*index=5*/bf16[256,512]{1,0:T(8,128)(2,1)}) fusion(f32[256,512]{1,0:T(8,128)S(1)} %get-tuple-element.24, f32[256]{0:T(256)S(1)} %add_rsqrt_fusion.1, f32[256]{0:T(256)S(1)} %broadcast_multiply_fusion.5, ...), kind=kLoop, calls=%fused_computation.54 | loop fusion | flops 11532800 | bytes 1586176 | tf_op jit(solution)/shard_map/reduce_sum | solution.py:113
  34.9 2.4 %fusion.42 = f32[1536,512]{1,0:T(8,128)} fusion(bf16[256,512]{1,0:T(8,128)(2,1)S(1)} %bitcast.40, bf16[256,1024]{1,0:T(8,128)(2,1)S(1)} %copy-done.2, f32[256,512]{1,0:T(8,128)S(1)} %get-tuple-element.15, f32[256,512]{1,0:T(8,128)S(1)} %get-tuple-element.24, f32[256]{0:T(256)S(1)} %get-tuple-element.25, f32[256]{0:T(256)S(1)} %get-tuple-element.26, ...), kind=kOutput, calls=%fused_computation.79 | convolution fusion | flops 405274624 | bytes 4986880 | tf_op jit(solution)/shard_map/dot_general | solution.py:119
  37.4 1.7 %fusion.51 = f32[256,1536]{1,0:T(8,128)S(1)} fusion(bf16[1536,512]{1,0:T(8,128)(2,1)S(1)} %copy-done, f32[256,512]{1,0:T(8,128)} %copy-done.1, f32[256,512]{1,0:T(8,128)S(1)} %get-tuple-element.24, f32[256]{0:T(256)S(1)} %get-tuple-element.25, f32[256]{0:T(256)S(1)} %get-tuple-element.26, f32[512]{0:T(512)S(1)} %copy-done.4, f32[256]{0:T(256)S(1)} %add_rsqrt_fusion.1, ...), kind=kOutput, calls=%fused_computation.106 | convolution fusion | flops 403701760 | bytes 4200448 | tf_op jit(solution)/shard_map/dot_general | solution.py:91
  39.2 5.0 %collective-permute-start.2 = (f32[4,1,512]{2,1,0:T(1,128)S(1)}, f32[4,1,512]{2,1,0:T(1,128)S(1)}, u32[]{:S(2)}, u32[]{:S(2)}) collective-permute-start(f32[4,1,512]{2,1,0:T(1,128)S(1)} %slice.52), channel_id=1, source_target_pairs={{0,1},{1,2},{2,3},{4,5},{5,6},{6,7},{8,9},{9,10},{10,11},{12,13},{... | collective-permute-start | bytes 24584 | tf_op jit(solution)/shard_map/ppermute | solution.py:14
  44.2 1.1 slice.50
  45.3 3.3 %reshape.143 = f32[4,64,2,512]{3,2,1,0:T(2,128)} reshape(f32[4,64,1024]{2,1,0:T(8,128)} %slice.50) | data formatting | bytes 2097152 | tf_op jit(solution)/shard_map/reshape | solution.py:94
  49.1 2.8 %slice_add_fusion = (f32[4,64,1,512]{3,2,1,0:T(1,128)S(1)}, f32[4,64,1,512]{3,2,1,0:T(1,128)S(1)}) fusion(f32[4,64,2,512]{3,2,1,0:T(2,128)} %reshape.143, f32[4,63,1,512]{3,2,1,0:T(1,128)S(1)} %copy.18, f32[4,1,1,512]{3,2,1,0:T(1,128)S(1)} %bitcast.45), kind=kLoop, calls=%fused_computation.52 | loop fusion | flops 262144 | bytes 2621440 | tf_op jit(solution)/shard_map/add | solution.py:97
  52.0 1.9 %pad_maximum_fusion = f32[4,64,2,512]{3,2,1,0:T(2,128)} fusion(f32[4,64,1,512]{3,2,1,0:T(1,128)S(1)} %get-tuple-element.17, f32[4,64,1,512]{3,2,1,0:T(1,128)S(1)} %get-tuple-element.16), kind=kLoop, calls=%fused_computation.10 | loop fusion | flops 262144 | bytes 2097152 | tf_op jit(solution)/shard_map/stack | solution.py:97
  53.9 2.9 %reshape_reshape.4 = f32[512,512]{1,0:T(8,128)} reshape(f32[4,64,2,512]{3,2,1,0:T(2,128)} %pad_maximum_fusion) | data formatting | bytes 2097152 | tf_op jit(solution)/shard_map/reshape;reshape | solution.py:100
  56.8 3.0 %multiply_reduce_fusion = (f32[512]{0:T(512)S(1)}, f32[512]{0:T(512)S(1)}, f32[512]{0:T(512)S(1)}, f32[512]{0:T(512)S(1)}, f32[512,512]{1,0:T(8,128)}) fusion(f32[512,512]{1,0:T(8,128)S(1)} %get-tuple-element.22, f32[512]{0:T(512)S(1)} %add_rsqrt_fusion, f32[512]{0:T(512)S(1)} %broadcast_multiply_fusion.2, f32[512]{0:T(512)S(1)} %copy-done.5, ...), kind=kLoop, calls=%fused_computation.11 | loop fusion | flops 5240832 | bytes 3162112 | tf_op jit(solution)/shard_map/reduce_sum | solution.py:111
  59.9 23.3 %reduce-scatter.2.cloned.1.call-done = f32[384,512]{1,0:T(8,128)} async-done(((f32[1536,512]{1,0:T(8,128)}), f32[384,512]{1,0:T(8,128)}) %reduce-scatter.2.cloned.1.call-update) | async-done | bytes 786448 | tf_op jit(solution)/shard_map/reduce_scatter | solution.py:118
  83.2 2.0 %fusion.8 = f32[10,512]{1,0:T(8,128)S(1)} fusion(bf16[512,10]{0,1:T(8,128)(2,1)S(1)} %bitcast.43, f32[512,512]{1,0:T(8,128)} %get-tuple-element.14, f32[512,512]{1,0:T(8,128)S(1)} %get-tuple-element.22, f32[512]{0:T(512)S(1)} %broadcast_multiply_fusion, f32[512]{0:T(512)S(1)} %broadcast_multiply_fusion.1, f32[512]{0:T(512)S(1)} %copy-done.5, ...), kind=kOutput, calls=%fused_computation.12 | convolution fusion | flops 33292288 | bytes 2138112 | tf_op jit(solution)/shard_map/dot_general | solution.py:102
  85.2 40.2 %all-reduce = (f32[10,512]{1,0:T(8,128)}, f32[4,512]{1,0:T(4,128)}) all-reduce(f32[10,512]{1,0:T(8,128)S(1)} %fusion.8, f32[4,512]{1,0:T(4,128)S(1)} %pad_maximum_fusion.5), channel_id=1, replica_groups=mesh['dp'=8,'seq'=4] {'dp','seq'}, use_global_device_ids=true, to_apply=%region_8.9 | all-reduce | flops 7168 | bytes 57344 | tf_op jit(solution)/shard_map/psum | solution.py:117
  125.4 17.9 %all-reduce.3.cloned.1.call-done = f32[384,512]{1,0:T(8,128)} async-done(((f32[384,512]{1,0:T(8,128)}), f32[384,512]{1,0:T(8,128)}) %all-reduce.3.cloned.1.call-update) | async-done | bytes 786448 | tf_op jit(solution)/shard_map/psum | solution.py:126
  143.3 2.1 %copy.21 = f32[384,512]{1,0:T(8,128)} copy(f32[384,512]{1,0:T(8,128)} %all-reduce.3.cloned.1.call-done) | data formatting | bytes 1572864
  (49 shorter events, 5.8 us)
Async XLA Ops:
  7.2 22.4 %copy-start = (bf16[1536,512]{1,0:T(8,128)(2,1)S(1)}, bf16[1536,512]{1,0:T(8,128)(2,1)}, u32[]{:S(2)}) copy-start(bf16[1536,512]{1,0:T(8,128)(2,1)} %param.12) | copy-start | bytes 4718596
  7.2 76.0 %reduce-scatter.2.cloned.1.call-start = ((), (), s32[]{:S(2)}) async-start(), calls=%async_computation.1 | async-start | bytes 3932160 | tf_op jit(solution)/shard_map/reduce_scatter | solution.py:118
  8.0 6.4 %collective-permute-start = (bf16[4,16]{1,0:T(4,128)(2,1)S(1)}, bf16[4,16]{1,0:T(4,128)(2,1)S(1)}, u32[]{:S(2)}, u32[]{:S(2)}) collective-permute-start(bf16[4,16]{1,0:T(4,128)(2,1)S(1)} %slice.36), channel_id=1, source_target_pairs={{1,0},{2,1},{3,2},{5,4},{6,5},{7,6},{9,8},{10,9},{11,10},{13,12},{... | collective-permute-start | bytes 392 | tf_op jit(solution)/shard_map/ppermute | solution.py:14
  15.1 2.0 %copy-start.5 = (f32[512]{0:T(512)S(1)}, f32[512]{0:T(512)}, u32[]{:S(2)}) copy-start(f32[512]{0:T(512)} %param.13) | copy-start | bytes 6148
  15.1 2.0 %copy-start.6 = (f32[512]{0:T(512)S(1)}, f32[512]{0:T(512)}, u32[]{:S(2)}) copy-start(f32[512]{0:T(512)} %param.14) | copy-start | bytes 6148
  20.1 6.4 %collective-permute-start.1 = (bf16[4,1,512]{2,1,0:T(2,128)(2,1)S(1)}, bf16[4,1,512]{2,1,0:T(2,128)(2,1)S(1)}, u32[]{:S(2)}, u32[]{:S(2)}) collective-permute-start(bf16[4,1,512]{2,1,0:T(2,128)(2,1)S(1)} %slice.49), channel_id=1, source_target_pairs={{1,0},{2,1},{3,2},{5,4},{6,5},{7,6},{9,8},{10,9},{11,10},{13,12},{... | collective-permute-start | bytes 12296 | tf_op jit(solution)/shard_map/ppermute | solution.py:14
  29.6 2.0 %copy-start.3 = (bf16[4,64,512]{2,1,0:T(8,128)(2,1)S(1)}, bf16[4,64,512]{2,1,0:T(8,128)(2,1)}, u32[]{:S(2)}) copy-start(bf16[4,64,512]{2,1,0:T(8,128)(2,1)} %param.17) | copy-start | bytes 786436
  29.6 2.0 %copy-start.4 = (f32[512]{0:T(512)S(1)}, f32[512]{0:T(512)}, u32[]{:S(2)}) copy-start(f32[512]{0:T(512)} %param.15) | copy-start | bytes 6148
  29.6 2.0 %copy-start.7 = (f32[512]{0:T(512)S(1)}, f32[512]{0:T(512)}, u32[]{:S(2)}) copy-start(f32[512]{0:T(512)} %param.16) | copy-start | bytes 6148
  31.3 3.6 %copy-start.2 = (bf16[256,1024]{1,0:T(8,128)(2,1)S(1)}, bf16[256,1024]{1,0:T(8,128)(2,1)}, u32[]{:S(2)}) copy-start(bf16[256,1024]{1,0:T(8,128)(2,1)} %concatenate.27) | copy-start | bytes 1572868
  34.1 0.8 copy-start.1
  37.4 105.9 %all-reduce.3.cloned.1.call-start = ((), (), s32[]{:S(2)}) async-start(), calls=%async_computation.2 | async-start | bytes 1572864 | tf_op jit(solution)/shard_map/psum | solution.py:126
  39.2 10.0 %collective-permute-start.2 = (f32[4,1,512]{2,1,0:T(1,128)S(1)}, f32[4,1,512]{2,1,0:T(1,128)S(1)}, u32[]{:S(2)}, u32[]{:S(2)}) collective-permute-start(f32[4,1,512]{2,1,0:T(1,128)S(1)} %slice.52), channel_id=1, source_target_pairs={{0,1},{1,2},{2,3},{4,5},{5,6},{6,7},{8,9},{9,10},{10,11},{12,13},{... | collective-permute-start | bytes 24584 | tf_op jit(solution)/shard_map/ppermute | solution.py:14
Sparse Core Ops, SparseCore 0:
  37.5 45.6 reduce-scatter.1
  85.5 57.7 all-reduce.2
where the time goes:
time: 153 us; the launch traced here: 152 us
  waiting for transfers between devices  49.6 us (32%)
  blocking collectives  40.2 us (26%)
  other arithmetic  16.1 us (11%)
  local copies, waits for them, and re-layouts  15.2 us (10%)
  between operations  14.3 us (9%)
  matrix products  8.97 us (6%)
  starting transfers between devices  7.65 us (5%)
    psum x1, blocking collectives, on_device(): grad_one_sum, norm_sum = lax.psum((grad_one, norm_terms), ('dp', 'seq'))  40.2 us
    reduce_scatter x1, waiting for transfers between devices, on_device(): lax.psum_scatter(lax.dot_general(patch_two, dpre_two, (((0,), (0,)), ((),...  23.3 us
    psum x1, waiting for transfers between devices, on_device(): grad_two = lax.psum(seq_share, 'dp')  17.9 us
    ppermute x3, waiting for transfers between devices, passed_along(): lax.ppermute(value, axis, [(source, source + steps) for source in range(f...  8.45 us
    ppermute x3, starting transfers between devices, passed_along(): lax.ppermute(value, axis, [(source, source + steps) for source in range(f...  7.57 us
    reshape x1, local copies, waits for them, and re-layouts, on_device(): dpatch_two[:, :, :2 * channels].reshape(clip_count, frames_two, 2, channels)  3.32 us
  transfers between devices with their start and end apart: 5, of which 4 were waited for; matrix products, arithmetic and copies ran while one was open for 14% of the time, Pallas kernels for 0%

commit v1 on v0

v1 whole, which is shorter than its diff:
```python
import functools

import jax
import jax.numpy as jnp
from jax import lax
from jax.experimental import pallas as pl
from jax.experimental.pallas import tpu as pltpu
from jax.sharding import PartitionSpec as P

MESH = pl.DeviceIdType.MESH
F32, BF16 = jnp.float32, jnp.bfloat16

epsilon = 1e-05
root_half = 0.7071067811865476
normal_peak = 0.3989422804014327

TAPS = 10
STEP = 32
PARTS = 2


def cdf(values):
    return 0.5 * (1.0 + lax.erf(values * root_half))


def slope_of(values, phi):
    return phi + values * jnp.exp(-0.5 * values * values) * normal_peak


def layer_norm(pre):
    centre = pre - jnp.mean(pre, axis=-1, keepdims=True)
    inverse = lax.rsqrt(jnp.mean(centre * centre, axis=-1, keepdims=True) + epsilon)
    return centre * inverse, inverse


def norm_backward(upstream, normed, inverse, gain):
    scaled = upstream * gain
    return inverse * (
        scaled
        - jnp.mean(scaled, axis=-1, keepdims=True)
        - normed * jnp.mean(scaled * normed, axis=-1, keepdims=True)
    )


def fold8(value):
    rows, channels = value.shape
    return jnp.sum(value.reshape(rows // 8, 8, channels), axis=0)


def dot_first(a, b):
    return lax.dot_general(a, b, (((0,), (0,)), ((), ())), preferred_element_type=F32)


def dot_last(a, b):
    return lax.dot_general(a, b, (((1,), (1,)), ((), ())), preferred_element_type=F32)


def kernel(
    ns, nz, pieces,
    wave, lengths, conv_one, conv_two, gain_one, shift_one, gain_two, shift_two, cot,
    features, grad_one_out, grad_two_out, norms_out,
    halo, patch, pre, hat, inv, phi, even, patch_two, pre_two, dpre_two, shifted, dact, dhi, dlo,
    mine, from_core, core_sum, from_seq, seq_sum, from_z, full,
    small, small_core, small_sum, small_seq, small_part, small_z,
    halo_s, halo_r, a_s, a_r, b_s, b_r, c_s, c_r, d_s, d_r, e_s, e_r,
    sa_s, sa_r, sb_s, sb_r, sc_s, sc_r,
):
    clips, samples = wave.shape
    channels = conv_two.shape[1]
    half = samples // (2 * 5)
    rows = clips * half
    share = mine.shape[3]
    width = mine.shape[4]
    piece = share // pieces

    pos = lax.axis_index("seq")
    dp = lax.axis_index("dp")
    z, core = dp // 2, lax.rem(dp, 2)
    partner = dp + 1 - 2 * core

    def at(dp_index, seq_index):
        return {"device_id": (dp_index, seq_index), "device_id_type": MESH}

    def seq_peer(d):
        return lax.rem(pos + d, ns)

    def z_peer(d):
        return lax.rem(z + d, nz)

    barrier = pltpu.get_barrier_semaphore()
    pl.semaphore_signal(barrier, inc=1, **at(partner, pos))
    for d in range(1, ns):
        pl.semaphore_signal(barrier, inc=1, **at(dp, seq_peer(d)))
    for d in range(1, nz):
        pl.semaphore_signal(barrier, inc=1, **at(2 * z_peer(d) + core, pos))

    g1, b1 = gain_one[...], shift_one[...]
    g2, b2 = gain_two[...], shift_two[...]
    taps = conv_one[...]

    def gather_frames(offset, source):
        total = source.shape[1]
        lane = lax.broadcasted_iota(jnp.int32, (half, total), 1) - offset - TAPS * lax.broadcasted_iota(
            jnp.int32, (half, total), 0
        )
        hit = (lane >= 0) & (lane < TAPS)
        picked = jnp.concatenate(
            [jnp.where(hit, source[c : c + 1, :], 0.0).astype(BF16) for c in range(clips)], axis=0
        )
        tap = lax.rem(
            lax.broadcasted_iota(jnp.int32, (total, 128), 0) + (TAPS - offset), TAPS
        )
        select = jnp.where(
            tap == lax.broadcasted_iota(jnp.int32, (total, 128), 1), 1.0, 0.0
        ).astype(BF16)
        return jnp.dot(picked, select, preferred_element_type=F32).astype(BF16)

    wave_f = wave[...].astype(F32)
    patch[0:rows] = gather_frames(0, wave_f)
    pre[0:rows] = jnp.dot(patch[0:rows, 0:TAPS], taps, preferred_element_type=F32)

    pl.semaphore_wait(barrier, ns + nz - 1)
    halo_copy = pltpu.make_async_remote_copy(
        wave.at[:, pl.ds(0, 128)], halo, halo_s, halo_r, **at(dp, lax.rem(pos + ns - 1, ns))
    )
    halo_copy.start()

    def forward_one(value):
        normed, inverse = layer_norm(value)
        out = normed * g1 + b1
        probability = cdf(out)
        return normed, inverse, probability, out * probability

    per_clip = half // STEP

    @pl.loop(0, rows // STEP)
    def _(i):
        r = pl.multiple_of(i * STEP, STEP)
        normed, inverse, probability, act = forward_one(pre[pl.ds(r, STEP)])
        hat[pl.ds(r, STEP)] = normed
        inv[pl.ds(r, STEP)] = jnp.broadcast_to(inverse, (STEP, 128))
        phi[pl.ds(r, STEP)] = probability
        even[i // per_clip, pl.ds(pl.multiple_of(lax.rem(i, per_clip) * STEP, STEP), STEP)] = act
        patch_two[pl.ds(r, STEP), pl.ds(0, channels)] = act.astype(BF16)

    halo_copy.wait()
    inside = jnp.where(pos < ns - 1, 1.0, 0.0).astype(F32)
    edge = (halo[...].astype(F32) * inside).astype(BF16)
    patch[rows : 2 * rows] = gather_frames(
        TAPS // 2, jnp.concatenate([wave_f, edge.astype(F32)], axis=1)
    )
    pre[rows : 2 * rows] = jnp.dot(patch[rows : 2 * rows, 0:TAPS], taps, preferred_element_type=F32)

    edge_pre = jnp.dot(edge[:, 0:TAPS], taps, preferred_element_type=F32)
    edge_hat, edge_inv, edge_phi, edge_act = forward_one(edge_pre)
    edge_act = edge_act * inside
    for c in range(clips):
        even[c, half : half + 1] = edge_act[c : c + 1]

    @pl.loop(rows // STEP, 2 * rows // STEP)
    def _(i):
        r = pl.multiple_of(i * STEP, STEP)
        normed, inverse, probability, act = forward_one(pre[pl.ds(r, STEP)])
        hat[pl.ds(r, STEP)] = normed
        inv[pl.ds(r, STEP)] = jnp.broadcast_to(inverse, (STEP, 128))
        phi[pl.ds(r, STEP)] = probability
        patch_two[pl.ds(pl.multiple_of(r - rows, STEP), STEP), pl.ds(channels, channels)] = act.astype(BF16)

    for c in range(clips):
        patch_two[c * half : (c + 1) * half, 2 * channels : 3 * channels] = even[
            c, 1 : half + 1
        ].astype(BF16)

    pre_two[...] = jnp.dot(patch_two[...], conv_two[...], preferred_element_type=F32)

    zeros8 = jnp.zeros((8, channels), F32)

    def second(i, sums):
        r = pl.multiple_of(i * STEP, STEP)
        normed, inverse = layer_norm(pre_two[pl.ds(r, STEP)])
        out = normed * g2 + b2
        probability = cdf(out)
        limit = lengths[0, i // per_clip] // 10 - 1
        frame = (
            pos * half
            + lax.rem(i, per_clip) * STEP
            + lax.broadcasted_iota(jnp.int32, (STEP, channels), 0)
        )
        valid = jnp.where(frame < limit, 1.0, 0.0).astype(F32)
        features[pl.ds(r, STEP)] = (out * probability * valid).astype(BF16)
        up = cot[pl.ds(r, STEP)].astype(F32) * valid * slope_of(out, probability)
        dpre_two[pl.ds(r, STEP)] = norm_backward(up, normed, inverse, g2).astype(BF16)
        return sums[0] + fold8(up * normed), sums[1] + fold8(up)

    two_hat, two_up = lax.fori_loop(0, rows // STEP, second, (zeros8, zeros8))

    down = dpre_two[...]
    for i in range(3 * channels // 384):
        product = dot_first(patch_two[:, i * 384 : (i + 1) * 384], down).astype(BF16)
        for j in range(384 // share):
            index = i * (384 // share) + j
            for q in range(PARTS):
                mine[q, index % 2, index // 2] = product[
                    j * share : (j + 1) * share, q * width : (q + 1) * width
                ]

    def core_copy(q):
        return pltpu.make_async_remote_copy(
            mine.at[q, 1 - core], from_core.at[q], a_s.at[q], a_r.at[q], **at(partner, pos)
        )

    def seq_copy(q, d):
        return pltpu.make_async_remote_copy(
            core_sum.at[q, d - 1], from_seq.at[q, d - 1], b_s.at[q, d - 1], b_r.at[q, d - 1],
            **at(dp, seq_peer(d)),
        )

    def z_rows(owner):
        return pl.ds(pl.multiple_of(owner * piece, piece), piece)

    def z_copy(q, d):
        return pltpu.make_async_remote_copy(
            seq_sum.at[q, z_rows(z_peer(d))], from_z.at[q, d - 1], c_s.at[q, d - 1], c_r.at[q, d - 1],
            **at(2 * z_peer(d) + core, pos),
        )

    def full_slice(q, which, owner):
        return full.at[q, which, z_rows(owner)]

    def spread_copy(q, d):
        there = full_slice(q, core, z)
        return pltpu.make_async_remote_copy(
            there, there, d_s.at[q, d - 1], d_r.at[q, d - 1], **at(2 * z_peer(d) + core, pos)
        )

    def relay_copy(q, d, which):
        there = full_slice(q, which, z_peer(d))
        return pltpu.make_async_remote_copy(
            there, there, e_s.at[q, d], e_r.at[q, d], **at(partner, pos)
        )

    def when_owner(owner, body):
        if pieces == nz:
            body()
        else:
            pl.when(owner < pieces)(body)

    for q in range(PARTS):
        core_copy(q).start()

    def to_seq(q):
        core_copy(q).wait()
        for d in range(1, ns):
            b = seq_peer(d)
            core_sum[q, d - 1] = (
                mine[q, core, b].astype(F32) + from_core[q, b].astype(F32)
            ).astype(BF16)
            seq_copy(q, d).start()

    def to_z(q):
        total = mine[q, core, pos].astype(F32) + from_core[q, pos].astype(F32)
        for d in range(1, ns):
            seq_copy(q, d).wait()
            total = total + from_seq[q, d - 1].astype(F32)
        seq_sum[q] = total.astype(BF16)
        for d in range(1, nz):
            when_owner(z_peer(d), lambda d=d: z_copy(q, d).start())

    def finish_z(q):
        def body():
            total = seq_sum[q, z_rows(z)].astype(F32)
            for d in range(1, nz):
                z_copy(q, d).wait_recv()
                total = total + from_z[q, d - 1].astype(F32)
            full[q, core, z_rows(z)] = total.astype(BF16)
            for d in range(1, nz):
                spread_copy(q, d).start()
            relay_copy(q, 0, core).start()

        when_owner(z, body)

    def relay(q):
        for d in range(1, nz):
            def body(d=d):
                spread_copy_from(q, d).wait_recv()
                relay_copy(q, nz - d, core).start()

            when_owner(z_peer(nz - d), body)

    def spread_copy_from(q, d):
        there = full_slice(q, core, z_peer(nz - d))
        return pltpu.make_async_remote_copy(
            there, there, d_s.at[q, d - 1], d_r.at[q, d - 1], **at(2 * z_peer(d) + core, pos)
        )

    for q in range(PARTS):
        to_seq(q)

    shifted[:, 0:8] = jnp.zeros((clips, 8, channels), F32)
    onward = dot_last(down, conv_two[2 * channels : 3 * channels])
    for c in range(clips):
        shifted[c, 8 : 8 + half] = onward[c * half : (c + 1) * half]
    first = dot_last(down, conv_two[0:channels])
    for c in range(clips):
        dact[c * half : (c + 1) * half] = first[c * half : (c + 1) * half] + shifted[c, 7 : 7 + half]
    dact[rows : 2 * rows] = dot_last(down, conv_two[channels : 2 * channels])

    def backward_one(incoming, normed, inverse, probability):
        up = incoming * slope_of(normed * g1 + b1, probability)
        return up, norm_backward(up, normed, inverse, g1)

    def back(i, sums):
        at_rows = pl.ds(pl.multiple_of(i * STEP, STEP), STEP)
        normed = hat[at_rows]
        up, dpre = backward_one(dact[at_rows], normed, inv[at_rows, 0:1], phi[at_rows])
        high = dpre.astype(BF16)
        dhi[at_rows] = high
        dlo[at_rows] = (dpre - high.astype(F32)).astype(BF16)
        return sums[0] + fold8(up * normed), sums[1] + fold8(up)

    one_hat, one_up = lax.fori_loop(0, 2 * rows // STEP, back, (zeros8, zeros8))

    edge_in = jnp.concatenate([shifted[c, 7 + half : 8 + half] for c in range(clips)], axis=0) * inside
    edge_up, edge_dpre = backward_one(edge_in, edge_hat, edge_inv, edge_phi)
    edge_high = edge_dpre.astype(BF16)
    edge_low = (edge_dpre - edge_high.astype(F32)).astype(BF16)

    frames = patch[...]
    grad_one = (
        dot_first(frames, dhi[...])
        + dot_first(frames, dlo[...])
    )[0:16] + (dot_first(edge, edge_high) + dot_first(edge, edge_low))[0:16]

    def total_row(value):
        return jnp.sum(value, axis=0, keepdims=True)

    small[...] = grad_one
    small[10:11] = total_row(one_hat) + total_row(edge_up * edge_hat)
    small[11:12] = total_row(one_up) + total_row(edge_up)
    small[12:13] = total_row(two_hat)
    small[13:14] = total_row(two_up)
    small[14:16] = jnp.zeros((2, channels), F32)

    small_core_copy = pltpu.make_async_remote_copy(small, small_core, sa_s, sa_r, **at(partner, pos))
    small_core_copy.start()

    def small_seq_copy(d):
        return pltpu.make_async_remote_copy(
            small_sum, small_seq.at[pos], sb_s.at[d - 1], sb_r.at[d - 1], **at(dp, seq_peer(d))
        )

    def small_z_copy(d):
        return pltpu.make_async_remote_copy(
            small_part, small_z.at[z], sc_s.at[d - 1], sc_r.at[d - 1], **at(2 * z_peer(d) + core, pos)
        )

    small_core_copy.wait()
    small_sum[...] = small[...] + small_core[...]
    for d in range(1, ns):
        small_seq_copy(d).start()
    small_seq[pos] = small_sum[...]

    to_z(0)

    for d in range(1, ns):
        small_seq_copy(d).wait()
    total = small_seq[0]
    for s in range(1, ns):
        total = total + small_seq[s]
    small_part[...] = total
    for d in range(1, nz):
        small_z_copy(d).start()
    small_z[z] = total

    for q in range(PARTS):
        if q > 0:
            to_z(q)
        finish_z(q)
    for q in range(PARTS):
        relay(q)

    for d in range(1, nz):
        small_z_copy(d).wait()
    total = small_z[0]
    for s in range(1, nz):
        total = total + small_z[s]
    grad_one_out[...] = total[0:TAPS]
    norms_out[...] = total[10:14]

    for q in range(PARTS):
        for d in range(1, nz):
            when_owner(z_peer(d), lambda d=d: z_copy(q, d).wait_send())

        def sent():
            for d in range(1, nz):
                spread_copy(q, d).wait_send()

        when_owner(z, sent)
        for d in range(nz):

            def relayed(d=d):
                relay_copy(q, d, core).wait_send()
                relay_copy(q, d, 1 - core).wait_recv()

            when_owner(z_peer(d), relayed)
        for h in range(2):
            grad_two_out[h * share : (h + 1) * share, q * width : (q + 1) * width] = full[q, h]


def on_device(ns, nz, waveform, lengths, conv_one, conv_two, gain_one, shift_one, gain_two, shift_two, cotangent):
    clips, samples = waveform.shape
    channels = conv_two.shape[1]
    half = cotangent.shape[1]
    rows = clips * half
    share = conv_two.shape[0] // ns // 2
    pieces = min(nz, share // 16)
    piece = share // pieces
    width = channels // PARTS
    dma = pltpu.SemaphoreType.DMA
    vmem = pl.BlockSpec(memory_space=pltpu.VMEM)
    features, grad_one, grad_two, norms = pl.pallas_call(
        functools.partial(kernel, ns, nz, pieces),
        out_shape=(
            jax.ShapeDtypeStruct((rows, channels), BF16),
            jax.ShapeDtypeStruct((TAPS, channels), F32),
            jax.ShapeDtypeStruct((2 * share, channels), BF16),
            jax.ShapeDtypeStruct((4, channels), F32),
        ),
        in_specs=[vmem, pl.BlockSpec(memory_space=pltpu.SMEM)] + [vmem] * 7,
        out_specs=(vmem,) * 4,
        scratch_shapes=[
            pltpu.VMEM((clips, 128), BF16),
            pltpu.VMEM((2 * rows, 128), BF16),
            pltpu.VMEM((2 * rows, channels), F32),
            pltpu.VMEM((2 * rows, channels), F32),
            pltpu.VMEM((2 * rows, 128), F32),
            pltpu.VMEM((2 * rows, channels), F32),
            pltpu.VMEM((clips, half + 8, channels), F32),
            pltpu.VMEM((rows, 3 * channels), BF16),
            pltpu.VMEM((rows, channels), F32),
            pltpu.VMEM((rows, channels), BF16),
            pltpu.VMEM((clips, half + 8, channels), F32),
            pltpu.VMEM((2 * rows, channels), F32),
            pltpu.VMEM((2 * rows, channels), BF16),
            pltpu.VMEM((2 * rows, channels), BF16),
            pltpu.VMEM((PARTS, 2, ns, share, width), BF16),
            pltpu.VMEM((PARTS, ns, share, width), BF16),
            pltpu.VMEM((PARTS, ns - 1, share, width), BF16),
            pltpu.VMEM((PARTS, ns - 1, share, width), BF16),
            pltpu.VMEM((PARTS, share, width), BF16),
            pltpu.VMEM((PARTS, nz - 1, piece, width), BF16),
            pltpu.VMEM((PARTS, 2, share, width), BF16),
            pltpu.VMEM((16, channels), F32),
            pltpu.VMEM((16, channels), F32),
            pltpu.VMEM((16, channels), F32),
            pltpu.VMEM((ns, 16, channels), F32),
            pltpu.VMEM((16, channels), F32),
            pltpu.VMEM((nz, 16, channels), F32),
            dma, dma,
            dma((PARTS,)), dma((PARTS,)),
            dma((PARTS, ns - 1)), dma((PARTS, ns - 1)),
            dma((PARTS, nz - 1)), dma((PARTS, nz - 1)),
            dma((PARTS, nz - 1)), dma((PARTS, nz - 1)),
            dma((PARTS, nz)), dma((PARTS, nz)),
            dma, dma,
            dma((ns - 1,)), dma((ns - 1,)),
            dma((nz - 1,)), dma((nz - 1,)),
        ],
        compiler_params=pltpu.CompilerParams(
            collective_id=0, has_side_effects=True, vmem_limit_bytes=48 * 1024 * 1024
        ),
    )(
        waveform,
        lengths,
        conv_one,
        conv_two,
        gain_one.reshape(1, channels),
        shift_one.reshape(1, channels),
        gain_two.reshape(1, channels),
        shift_two.reshape(1, channels),
        cotangent.reshape(rows, channels),
    )
    return features.reshape(clips, half, channels), grad_one, grad_two.astype(F32), norms


def solution(mesh):
    in_specs = (P("dp", "seq"), P("dp", None), P(), P(), P(), P(), P(), P(), P("dp", "seq", None))
    out_specs = (P("dp", "seq", None), P(), P("seq", None), P())
    return jax.shard_map(
        functools.partial(on_device, mesh.shape["seq"], mesh.shape["dp"] // 2),
        mesh=mesh, in_specs=in_specs, out_specs=out_specs, check_vma=False,
    )
```

time: 153 us -> 54.7 us (0.36)
  waiting for transfers between devices: 49.6 us -> 0 us
  Pallas kernels: 0 us -> 43.6 us
  blocking collectives: 40.2 us -> 0 us
  other arithmetic: 16.1 us -> 0.97 us
  between operations: 14.3 us -> 0.66 us
  matrix products: 8.97 us -> 0 us
  starting transfers between devices: 7.65 us -> 0 us
  local copies, waits for them, and re-layouts: 15.2 us -> 9.05 us
    pallas_call x0 -> x1, Pallas kernels: none -> 43.6 us  [on_device(): pl.pallas_call(functools.partial(kernel, ns, nz, pieces), out_shape=(jax....]
    psum x1 -> x0, blocking collectives: 40.2 us -> none  [on_device(): grad_one_sum, norm_sum = lax.psum((grad_one, norm_terms), ('dp', 'seq'))]
    reduce_scatter x1 -> x0, waiting for transfers between devices: 23.3 us -> none  [on_device(): lax.psum_scatter(lax.dot_general(patch_two, dpre_two, (((0,), (0,)), ((),...]
    psum x1 -> x0, waiting for transfers between devices: 17.9 us -> none  [on_device(): grad_two = lax.psum(seq_share, 'dp')]
    dot_general x5 -> x0, matrix products: 8.97 us -> none  [the longest x1 2.44 us: on_device(): lax.dot_general(patch_two, dpre_two, (((0,), (0,)), ((), ())), preferred_...]
    ppermute x3 -> x0, waiting for transfers between devices: 8.45 us -> none  [passed_along(): lax.ppermute(value, axis, [(source, source + steps) for source in range(f...]
    ppermute x3 -> x0, starting transfers between devices: 7.57 us -> none  [passed_along(): lax.ppermute(value, axis, [(source, source + steps) for source in range(f...]
    unnamed x19 -> x21, local copies, waits for them, and re-layouts: 2.9 us -> 9.05 us
  transfers between devices with their start and end apart: 5 -> 0, of which waited for: 4 -> 0; matrix products, arithmetic and copies ran while one was open for 14% -> 0% of each run, Pallas kernels for 0% -> 0%
where the time goes in v1:
time: 54.7 us; the launch traced here: 54.3 us
  Pallas kernels  43.6 us (80%)
  local copies, waits for them, and re-layouts  9.05 us (17%)
  other arithmetic  0.97 us (2%)
  between operations  0.66 us (1%)
    pallas_call x1, Pallas kernels, on_device(): pl.pallas_call(functools.partial(kernel, ns, nz, pieces), out_shape=(jax....  43.6 us
    unnamed x21, local copies, waits for them, and re-layouts  9.05 us

profile of v1, /device:TPU:0, one launch (start us, length us, event | category | flops | bytes accessed | tf_op | source)
XLA Modules:
  0.0 54.3 jit_solution(4799377311297748393)
XLA Ops:
  0.6 0.0 copy-start
  0.6 1.4 %copy-done = bf16[1536,512]{1,0:T(8,128)(2,1)S(1)} copy-done((bf16[1536,512]{1,0:T(8,128)(2,1)S(1)}, bf16[1536,512]{1,0:T(8,128)(2,1)}, u32[]{:S(2)}) %copy-start) | copy-done | bytes 1572888
  2.0 0.0 copy-start.1
  2.0 0.9 %copy-done.1 = bf16[4,64,512]{2,1,0:T(8,128)(2,1)S(1)} copy-done((bf16[4,64,512]{2,1,0:T(8,128)(2,1)S(1)}, bf16[4,64,512]{2,1,0:T(8,128)(2,1)}, u32[]{:S(2)}) %copy-start.1) | copy-done | bytes 262168
  3.0 0.0 copy-start.2
  3.0 0.7 %copy-done.2 = bf16[10,512]{1,0:T(8,128)(2,1)S(1)} copy-done((bf16[10,512]{1,0:T(8,128)(2,1)S(1)}, bf16[10,512]{1,0:T(8,128)(2,1)}, u32[]{:S(2)}) %copy-start.2) | copy-done | bytes 10264
  3.7 0.0 copy-start.3
  3.7 0.7 %copy-done.3 = bf16[4,640]{1,0:T(4,128)(2,1)S(1)} copy-done((bf16[4,640]{1,0:T(4,128)(2,1)S(1)}, bf16[4,640]{1,0:T(4,128)(2,1)}, u32[]{:S(2)}) %copy-start.3) | copy-done | bytes 5144
  4.4 0.0 copy-start.4
  4.4 0.7 %copy-done.4 = f32[512]{0:T(512)S(1)} copy-done((f32[512]{0:T(512)S(1)}, f32[512]{0:T(512)}, u32[]{:S(2)}) %copy-start.4) | copy-done | bytes 2072
  5.1 0.0 copy-start.5
  5.1 0.7 %copy-done.5 = f32[512]{0:T(512)S(1)} copy-done((f32[512]{0:T(512)S(1)}, f32[512]{0:T(512)}, u32[]{:S(2)}) %copy-start.5) | copy-done | bytes 2072
  5.8 0.0 copy-start.6
  5.8 0.7 %copy-done.6 = f32[512]{0:T(512)S(1)} copy-done((f32[512]{0:T(512)S(1)}, f32[512]{0:T(512)}, u32[]{:S(2)}) %copy-start.6) | copy-done | bytes 2072
  6.4 0.0 copy-start.7
  6.5 0.7 %copy-done.7 = f32[512]{0:T(512)S(1)} copy-done((f32[512]{0:T(512)S(1)}, f32[512]{0:T(512)}, u32[]{:S(2)}) %copy-start.7) | copy-done | bytes 2072
  7.1 0.0 copy-start.8
  7.1 0.7 %copy-done.8 = s32[1,4]{1,0:T(1,128)S(1)} copy-done((s32[1,4]{1,0:T(1,128)S(1)}, s32[1,4]{1,0:T(1,128)}, u32[]{:S(2)}) %copy-start.8) | copy-done | bytes 40
  7.8 43.6 %shard_map.120 = (bf16[256,512]{1,0:T(8,128)(2,1)S(1)}, f32[10,512]{1,0:T(8,128)S(1)}, bf16[384,512]{1,0:T(8,128)(2,1)S(1)}, f32[4,512]{1,0:T(4,128)S(1)}) custom-call(bf16[4,640]{1,0:T(4,128)(2,1)S(1)} %copy-done.3, s32[1,4]{1,0:T(1,128)S(1)} %copy-done.8, bf16[10,512]{1,0:T(8,128)(2,1)S(1)} %copy-done.2, bf16[1536,512]{1,0:T(8,128)(2,1)S(1)} %copy-done, ...), custom_call_target="tpu_custom_call" | custom-call | tf_op jit(solution)/shard_map/pallas_call | solution.py:421
  51.4 1.0 %convert_element_type.3 = f32[384,512]{1,0:T(8,128)} convert(bf16[384,512]{1,0:T(8,128)(2,1)S(1)} %get-tuple-element.10) | non-fusion elementwise | flops 196608 | bytes 1179648 | tf_op jit(solution)/shard_map/convert_element_type | solution.py:483
  52.4 0.7 %copy.16 = bf16[4,64,512]{2,1,0:T(8,128)(2,1)} copy(bf16[4,64,512]{2,1,0:T(8,128)(2,1)S(1)} %bitcast.6) | data formatting | bytes 524288
  53.1 0.6 %copy.17 = f32[10,512]{1,0:T(8,128)} copy(f32[10,512]{1,0:T(8,128)S(1)} %get-tuple-element.17) | data formatting | bytes 40960
  53.7 0.6 %copy.18 = f32[4,512]{1,0:T(4,128)} copy(f32[4,512]{1,0:T(4,128)S(1)} %get-tuple-element.19) | data formatting | bytes 16384
Async XLA Ops:
  0.6 1.4 %copy-start = (bf16[1536,512]{1,0:T(8,128)(2,1)S(1)}, bf16[1536,512]{1,0:T(8,128)(2,1)}, u32[]{:S(2)}) copy-start(bf16[1536,512]{1,0:T(8,128)(2,1)} %conv_two.1) | copy-start | bytes 4718596
  2.0 0.9 %copy-start.1 = (bf16[4,64,512]{2,1,0:T(8,128)(2,1)S(1)}, bf16[4,64,512]{2,1,0:T(8,128)(2,1)}, u32[]{:S(2)}) copy-start(bf16[4,64,512]{2,1,0:T(8,128)(2,1)} %param.17) | copy-start | bytes 786436
  3.0 0.7 %copy-start.2 = (bf16[10,512]{1,0:T(8,128)(2,1)S(1)}, bf16[10,512]{1,0:T(8,128)(2,1)}, u32[]{:S(2)}) copy-start(bf16[10,512]{1,0:T(8,128)(2,1)} %conv_one.1) | copy-start | bytes 30724
  3.7 0.7 %copy-start.3 = (bf16[4,640]{1,0:T(4,128)(2,1)S(1)}, bf16[4,640]{1,0:T(4,128)(2,1)}, u32[]{:S(2)}) copy-start(bf16[4,640]{1,0:T(4,128)(2,1)} %wave.1) | copy-start | bytes 15364
  4.4 0.7 %copy-start.4 = (f32[512]{0:T(512)S(1)}, f32[512]{0:T(512)}, u32[]{:S(2)}) copy-start(f32[512]{0:T(512)} %param.13) | copy-start | bytes 6148
  5.1 0.7 %copy-start.5 = (f32[512]{0:T(512)S(1)}, f32[512]{0:T(512)}, u32[]{:S(2)}) copy-start(f32[512]{0:T(512)} %param.14) | copy-start | bytes 6148
  5.8 0.7 %copy-start.6 = (f32[512]{0:T(512)S(1)}, f32[512]{0:T(512)}, u32[]{:S(2)}) copy-start(f32[512]{0:T(512)} %param.15) | copy-start | bytes 6148
  6.4 0.7 %copy-start.7 = (f32[512]{0:T(512)S(1)}, f32[512]{0:T(512)}, u32[]{:S(2)}) copy-start(f32[512]{0:T(512)} %param.16) | copy-start | bytes 6148
  7.1 0.7 %copy-start.8 = (s32[1,4]{1,0:T(1,128)S(1)}, s32[1,4]{1,0:T(1,128)}, u32[]{:S(2)}) copy-start(s32[1,4]{1,0:T(1,128)} %lengths.1) | copy-start | bytes 52

commit v2 on v1

--- a/solution.py
+++ b/solution.py
@@ -57,8 +57,9 @@
 
 def kernel(
     ns, nz, pieces,
-    wave, lengths, conv_one, conv_two, gain_one, shift_one, gain_two, shift_two, cot,
+    wave_in, lengths_in, conv_one_in, conv_two_in, gain_one_in, shift_one_in, gain_two_in, shift_two_in, cot_in,
     features, grad_one_out, grad_two_out, norms_out,
+    wave, lengths, conv_one, conv_two, gain_one, shift_one, gain_two, shift_two, cot, in_s,
     halo, patch, pre, hat, inv, phi, even, patch_two, pre_two, dpre_two, shifted, dact, dhi, dlo,
     mine, from_core, core_sum, from_seq, seq_sum, from_z, full,
     small, small_core, small_sum, small_seq, small_part, small_z,
@@ -87,6 +88,24 @@
     def z_peer(d):
         return lax.rem(z + d, nz)
 
+    loads = [
+        pltpu.make_async_copy(source, target, in_s.at[i])
+        for i, (source, target) in enumerate(
+            (
+                (wave_in, wave),
+                (conv_one_in, conv_one),
+                (gain_one_in, gain_one),
+                (shift_one_in, shift_one),
+                (conv_two_in, conv_two),
+                (gain_two_in, gain_two),
+                (shift_two_in, shift_two),
+                (lengths_in, lengths),
+                (cot_in, cot),
+            )
+        )
+    ]
+    for load in loads:
+        load.start()
     barrier = pltpu.get_barrier_semaphore()
     pl.semaphore_signal(barrier, inc=1, **at(partner, pos))
     for d in range(1, ns):
@@ -94,8 +113,9 @@
     for d in range(1, nz):
         pl.semaphore_signal(barrier, inc=1, **at(2 * z_peer(d) + core, pos))
 
+    for load in loads[:4]:
+        load.wait()
     g1, b1 = gain_one[...], shift_one[...]
-    g2, b2 = gain_two[...], shift_two[...]
     taps = conv_one[...]
 
     def gather_frames(offset, source):
@@ -113,11 +133,15 @@
         select = jnp.where(
             tap == lax.broadcasted_iota(jnp.int32, (total, 128), 1), 1.0, 0.0
         ).astype(BF16)
-        return jnp.dot(picked, select, preferred_element_type=F32).astype(BF16)
+        return jnp.dot(picked, select, preferred_element_type=F32)
 
     wave_f = wave[...].astype(F32)
-    patch[0:rows] = gather_frames(0, wave_f)
-    pre[0:rows] = jnp.dot(patch[0:rows, 0:TAPS], taps, preferred_element_type=F32)
+    for parity in range(2):
+        found = gather_frames(parity * TAPS // 2, wave_f)
+        patch[parity * rows : (parity + 1) * rows] = found
+        pre[parity * rows : (parity + 1) * rows] = jnp.dot(
+            found.astype(BF16)[:, 0:TAPS], taps, preferred_element_type=F32
+        )
 
     pl.semaphore_wait(barrier, ns + nz - 1)
     halo_copy = pltpu.make_async_remote_copy(
@@ -143,13 +167,33 @@
         even[i // per_clip, pl.ds(pl.multiple_of(lax.rem(i, per_clip) * STEP, STEP), STEP)] = act
         patch_two[pl.ds(r, STEP), pl.ds(0, channels)] = act.astype(BF16)
 
+    def odd_rows(block):
+        r = pl.multiple_of(rows + block * STEP, STEP)
+        normed, inverse, probability, act = forward_one(pre[pl.ds(r, STEP)])
+        hat[pl.ds(r, STEP)] = normed
+        inv[pl.ds(r, STEP)] = jnp.broadcast_to(inverse, (STEP, 128))
+        phi[pl.ds(r, STEP)] = probability
+        patch_two[pl.ds(pl.multiple_of(block * STEP, STEP), STEP), pl.ds(channels, channels)] = act.astype(BF16)
+
+    @pl.loop(0, clips * (per_clip - 1))
+    def _(i):
+        odd_rows(i // (per_clip - 1) * per_clip + lax.rem(i, per_clip - 1))
+
     halo_copy.wait()
     inside = jnp.where(pos < ns - 1, 1.0, 0.0).astype(F32)
     edge = (halo[...].astype(F32) * inside).astype(BF16)
-    patch[rows : 2 * rows] = gather_frames(
-        TAPS // 2, jnp.concatenate([wave_f, edge.astype(F32)], axis=1)
+    moved = lax.broadcasted_iota(jnp.int32, (128, 128), 0) + TAPS // 2
+    tap = lax.broadcasted_iota(jnp.int32, (128, 128), 1)
+    fix = jnp.dot(
+        edge,
+        jnp.where((moved == tap) & (tap < TAPS), 1.0, 0.0).astype(BF16),
+        preferred_element_type=F32,
     )
-    pre[rows : 2 * rows] = jnp.dot(patch[rows : 2 * rows, 0:TAPS], taps, preferred_element_type=F32)
+    fix_pre = jnp.dot(fix.astype(BF16)[:, 0:TAPS], taps, preferred_element_type=F32)
+    for c in range(clips):
+        last = rows + (c + 1) * half - 1
+        patch[last : last + 1] = patch[last : last + 1] + fix[c : c + 1]
+        pre[last : last + 1] = pre[last : last + 1] + fix_pre[c : c + 1]
 
     edge_pre = jnp.dot(edge[:, 0:TAPS], taps, preferred_element_type=F32)
     edge_hat, edge_inv, edge_phi, edge_act = forward_one(edge_pre)
@@ -157,20 +201,18 @@
     for c in range(clips):
         even[c, half : half + 1] = edge_act[c : c + 1]
 
-    @pl.loop(rows // STEP, 2 * rows // STEP)
-    def _(i):
-        r = pl.multiple_of(i * STEP, STEP)
-        normed, inverse, probability, act = forward_one(pre[pl.ds(r, STEP)])
-        hat[pl.ds(r, STEP)] = normed
-        inv[pl.ds(r, STEP)] = jnp.broadcast_to(inverse, (STEP, 128))
-        phi[pl.ds(r, STEP)] = probability
-        patch_two[pl.ds(pl.multiple_of(r - rows, STEP), STEP), pl.ds(channels, channels)] = act.astype(BF16)
+    @pl.loop(0, clips)
+    def _(c):
+        odd_rows(c * per_clip + per_clip - 1)
 
     for c in range(clips):
         patch_two[c * half : (c + 1) * half, 2 * channels : 3 * channels] = even[
             c, 1 : half + 1
         ].astype(BF16)
 
+    for load in loads[4:]:
+        load.wait()
+    g2, b2 = gain_two[...], shift_two[...]
     pre_two[...] = jnp.dot(patch_two[...], conv_two[...], preferred_element_type=F32)
 
     zeros8 = jnp.zeros((8, channels), F32)
@@ -325,7 +367,7 @@
     edge_high = edge_dpre.astype(BF16)
     edge_low = (edge_dpre - edge_high.astype(F32)).astype(BF16)
 
-    frames = patch[...]
+    frames = patch[...].astype(BF16)
     grad_one = (
         dot_first(frames, dhi[...])
         + dot_first(frames, dlo[...])
@@ -372,12 +414,13 @@
         small_z_copy(d).start()
     small_z[z] = total
 
-    for q in range(PARTS):
-        if q > 0:
+    for q in range(1, PARTS + 2):
+        if q < PARTS:
             to_z(q)
-        finish_z(q)
-    for q in range(PARTS):
-        relay(q)
+        if q - 1 < PARTS:
+            finish_z(q - 1)
+        if q > 1:
+            relay(q - 2)
 
     for d in range(1, nz):
         small_z_copy(d).wait()
@@ -418,6 +461,7 @@
     width = channels // PARTS
     dma = pltpu.SemaphoreType.DMA
     vmem = pl.BlockSpec(memory_space=pltpu.VMEM)
+    hbm = pl.BlockSpec(memory_space=pltpu.HBM)
     features, grad_one, grad_two, norms = pl.pallas_call(
         functools.partial(kernel, ns, nz, pieces),
         out_shape=(
@@ -426,11 +470,21 @@
             jax.ShapeDtypeStruct((2 * share, channels), BF16),
             jax.ShapeDtypeStruct((4, channels), F32),
         ),
-        in_specs=[vmem, pl.BlockSpec(memory_space=pltpu.SMEM)] + [vmem] * 7,
+        in_specs=[hbm] * 9,
         out_specs=(vmem,) * 4,
         scratch_shapes=[
+            pltpu.VMEM(waveform.shape, BF16),
+            pltpu.SMEM(lengths.shape, jnp.int32),
+            pltpu.VMEM(conv_one.shape, BF16),
+            pltpu.VMEM(conv_two.shape, BF16),
+            pltpu.VMEM((1, channels), F32),
+            pltpu.VMEM((1, channels), F32),
+            pltpu.VMEM((1, channels), F32),
+            pltpu.VMEM((1, channels), F32),
+            pltpu.VMEM((rows, channels), BF16),
+            dma((9,)),
             pltpu.VMEM((clips, 128), BF16),
-            pltpu.VMEM((2 * rows, 128), BF16),
+            pltpu.VMEM((2 * rows, 128), F32),
             pltpu.VMEM((2 * rows, channels), F32),
             pltpu.VMEM((2 * rows, channels), F32),
             pltpu.VMEM((2 * rows, 128), F32),
@@ -470,6 +524,9 @@
             collective_id=0, has_side_effects=True, vmem_limit_bytes=48 * 1024 * 1024
         ),
     )(
+        *[
+            pltpu.with_memory_space_constraint(value, pltpu.HBM)
+            for value in (
         waveform,
         lengths,
         conv_one,
@@ -479,8 +536,41 @@
         gain_two.reshape(1, channels),
         shift_two.reshape(1, channels),
         cotangent.reshape(rows, channels),
-    )
-    return features.reshape(clips, half, channels), grad_one, grad_two.astype(F32), norms
+    )])
+    features, grad_one, grad_two, norms = pl.pallas_call(
+        put_out,
+        out_shape=(
+            jax.ShapeDtypeStruct((rows, channels), BF16),
+            jax.ShapeDtypeStruct((TAPS, channels), F32),
+            jax.ShapeDtypeStruct((2 * share, channels), F32),
+            jax.ShapeDtypeStruct((4, channels), F32),
+        ),
+        in_specs=[vmem] * 4,
+        out_specs=(hbm,) * 4,
+        scratch_shapes=[pltpu.VMEM((2 * share, channels), F32), dma((4,))],
+        compiler_params=pltpu.CompilerParams(vmem_limit_bytes=4 * 1024 * 1024),
+    )(features, grad_one, grad_two, norms)
+    return features.reshape(clips, half, channels), grad_one, grad_two, norms
+
+
+def put_out(features, grad_one, grad_two, norms, features_out, grad_one_out, grad_two_out, norms_out, wide, sem):
+    copies = [
+        pltpu.make_async_copy(source, target, sem.at[i])
+        for i, (source, target) in enumerate(
+            (
+                (features, features_out),
+                (grad_one, grad_one_out),
+                (norms, norms_out),
+                (wide, grad_two_out),
+            )
+        )
+    ]
+    for copy in copies[:3]:
+        copy.start()
+    wide[...] = grad_two[...].astype(F32)
+    copies[3].start()
+    for copy in copies:
+        copy.wait()
 
 
 def solution(mesh):

time: 54.7 us -> 43.5 us (0.80)
  local copies, waits for them, and re-layouts: 9.05 us -> 0 us
  Pallas kernels: 43.6 us -> 42.6 us
  other arithmetic: 0.97 us -> 0 us
    unnamed x21 -> x0, local copies, waits for them, and re-layouts: 9.05 us -> none
    pallas_call x1, Pallas kernels: 43.6 us -> 41.6 us  [on_device(): pl.pallas_call(functools.partial(kernel, ns, nz, pieces), out_shape=(jax....]
    pallas_call x0 -> x1, Pallas kernels: none -> 1.02 us  [on_device(): pl.pallas_call(put_out, out_shape=(jax.ShapeDtypeStruct((rows, channels),...]
    convert_element_type x1 -> x0, other arithmetic: 0.97 us -> none  [on_device(): grad_two.astype(F32)]
where the time goes in v2:
time: 43.5 us; the launch traced here: 43.3 us
  Pallas kernels  42.6 us (98%)
  between operations  0.64 us (1%)
    pallas_call x1, Pallas kernels, on_device(): pl.pallas_call(functools.partial(kernel, ns, nz, pieces), out_shape=(jax....  41.6 us
    pallas_call x1, Pallas kernels, on_device(): pl.pallas_call(put_out, out_shape=(jax.ShapeDtypeStruct((rows, channels),...  1.02 us

profile of v2, /device:TPU:0, one launch (start us, length us, event | category | flops | bytes accessed | tf_op | source)
XLA Modules:
  0.0 43.3 jit_solution(5232238129617316455)
XLA Ops:
  0.6 41.6 %shard_map.120 = (bf16[256,512]{1,0:T(8,128)(2,1)S(1)}, f32[10,512]{1,0:T(8,128)S(1)}, bf16[384,512]{1,0:T(8,128)(2,1)S(1)}, f32[4,512]{1,0:T(4,128)S(1)}) custom-call(bf16[4,640]{1,0:T(4,128)(2,1)} %wave_in.1, s32[1,4]{1,0:T(1,128)} %lengths_in.1, bf16[10,512]{1,0:T(8,128)(2,1)} %conv_one_in.1, bf16[1536,512]{1,0:T(8,128)(2,1)} %conv_two_in.1, ...), custom_call_target="tpu_custom_call" | custom-call | tf_op jit(solution)/shard_map/pallas_call | solution.py:465
  42.2 1.0 %shard_map.121 = (bf16[256,512]{1,0:T(8,128)(2,1)}, f32[10,512]{1,0:T(8,128)}, f32[384,512]{1,0:T(8,128)}, f32[4,512]{1,0:T(4,128)}) custom-call(bf16[256,512]{1,0:T(8,128)(2,1)S(1)} %get-tuple-element.12.features, f32[10,512]{1,0:T(8,128)S(1)} %get-tuple-element.13.grad_one, bf16[384,512]{1,0:T(8,128)(2,1)S(1)} %get-tuple-element.14.grad_two, ...), custom_call_target="tpu_custom_call" | custom-call | tf_op jit(solution)/shard_map/pallas_call | solution.py:540

commit v3 on v2

--- a/solution.py
+++ b/solution.py
@@ -62,9 +62,9 @@
     wave, lengths, conv_one, conv_two, gain_one, shift_one, gain_two, shift_two, cot, in_s,
     halo, patch, pre, hat, inv, phi, even, patch_two, pre_two, dpre_two, shifted, dact, dhi, dlo,
     mine, from_core, core_sum, from_seq, seq_sum, from_z, full,
-    small, small_core, small_sum, small_seq, small_part, small_z,
+    small, small_core, small_sum, small_seq, small_part, small_z, small_all,
     halo_s, halo_r, a_s, a_r, b_s, b_r, c_s, c_r, d_s, d_r, e_s, e_r,
-    sa_s, sa_r, sb_s, sb_r, sc_s, sc_r,
+    sa_s, sa_r, sb_s, sb_r, sc_s, sc_r, sd_s, sd_r,
 ):
     clips, samples = wave.shape
     channels = conv_two.shape[1]
@@ -143,12 +143,6 @@
             found.astype(BF16)[:, 0:TAPS], taps, preferred_element_type=F32
         )
 
-    pl.semaphore_wait(barrier, ns + nz - 1)
-    halo_copy = pltpu.make_async_remote_copy(
-        wave.at[:, pl.ds(0, 128)], halo, halo_s, halo_r, **at(dp, lax.rem(pos + ns - 1, ns))
-    )
-    halo_copy.start()
-
     def forward_one(value):
         normed, inverse = layer_norm(value)
         out = normed * g1 + b1
@@ -157,8 +151,7 @@
 
     per_clip = half // STEP
 
-    @pl.loop(0, rows // STEP)
-    def _(i):
+    def even_rows(i):
         r = pl.multiple_of(i * STEP, STEP)
         normed, inverse, probability, act = forward_one(pre[pl.ds(r, STEP)])
         hat[pl.ds(r, STEP)] = normed
@@ -166,6 +159,17 @@
         phi[pl.ds(r, STEP)] = probability
         even[i // per_clip, pl.ds(pl.multiple_of(lax.rem(i, per_clip) * STEP, STEP), STEP)] = act
         patch_two[pl.ds(r, STEP), pl.ds(0, channels)] = act.astype(BF16)
+
+    blocks = rows // STEP
+    pl.loop(0, blocks // 2)(even_rows)
+
+    pl.semaphore_wait(barrier, ns + nz - 1)
+    halo_copy = pltpu.make_async_remote_copy(
+        wave.at[:, pl.ds(0, 128)], halo, halo_s, halo_r, **at(dp, lax.rem(pos + ns - 1, ns))
+    )
+    halo_copy.start()
+
+    pl.loop(blocks // 2, blocks)(even_rows)
 
     def odd_rows(block):
         r = pl.multiple_of(rows + block * STEP, STEP)
@@ -237,18 +241,10 @@
     two_hat, two_up = lax.fori_loop(0, rows // STEP, second, (zeros8, zeros8))
 
     down = dpre_two[...]
-    for i in range(3 * channels // 384):
-        product = dot_first(patch_two[:, i * 384 : (i + 1) * 384], down).astype(BF16)
-        for j in range(384 // share):
-            index = i * (384 // share) + j
-            for q in range(PARTS):
-                mine[q, index % 2, index // 2] = product[
-                    j * share : (j + 1) * share, q * width : (q + 1) * width
-                ]
-
-    def core_copy(q):
-        return pltpu.make_async_remote_copy(
-            mine.at[q, 1 - core], from_core.at[q], a_s.at[q], a_r.at[q], **at(partner, pos)
+    def core_copy(q, d):
+        b = seq_peer(d)
+        return pltpu.make_async_remote_copy(
+            mine.at[q, 1 - core, b], from_core.at[q, b], a_s.at[q, d], a_r.at[q, d], **at(partner, pos)
         )
 
     def seq_copy(q, d):
@@ -288,18 +284,27 @@
             pl.when(owner < pieces)(body)
 
     for q in range(PARTS):
-        core_copy(q).start()
+        for i in range(3 * channels // 384):
+            product = dot_first(
+                patch_two[:, i * 384 : (i + 1) * 384], down[:, q * width : (q + 1) * width]
+            ).astype(BF16)
+            for j in range(384 // share):
+                index = i * (384 // share) + j
+                mine[q, index % 2, index // 2] = product[j * share : (j + 1) * share]
+        for d in [*range(1, ns), 0]:
+            core_copy(q, d).start()
 
     def to_seq(q):
-        core_copy(q).wait()
         for d in range(1, ns):
             b = seq_peer(d)
+            core_copy(q, d).wait()
             core_sum[q, d - 1] = (
                 mine[q, core, b].astype(F32) + from_core[q, b].astype(F32)
             ).astype(BF16)
             seq_copy(q, d).start()
 
     def to_z(q):
+        core_copy(q, 0).wait()
         total = mine[q, core, pos].astype(F32) + from_core[q, pos].astype(F32)
         for d in range(1, ns):
             seq_copy(q, d).wait()
@@ -376,14 +381,22 @@
     def total_row(value):
         return jnp.sum(value, axis=0, keepdims=True)
 
-    small[...] = grad_one
-    small[10:11] = total_row(one_hat) + total_row(edge_up * edge_hat)
-    small[11:12] = total_row(one_up) + total_row(edge_up)
-    small[12:13] = total_row(two_hat)
-    small[13:14] = total_row(two_up)
-    small[14:16] = jnp.zeros((2, channels), F32)
-
-    small_core_copy = pltpu.make_async_remote_copy(small, small_core, sa_s, sa_r, **at(partner, pos))
+    middle = channels // 2
+    sums = (
+        (0, grad_one),
+        (10, total_row(one_hat) + total_row(edge_up * edge_hat)),
+        (11, total_row(one_up) + total_row(edge_up)),
+        (12, total_row(two_hat)),
+        (13, total_row(two_up)),
+        (14, jnp.zeros((2, channels), F32)),
+    )
+    for row, value in sums:
+        for h in range(2):
+            small[h, row : row + value.shape[0]] = value[:, h * middle : (h + 1) * middle]
+
+    small_core_copy = pltpu.make_async_remote_copy(
+        small.at[1 - core], small_core, sa_s, sa_r, **at(partner, pos)
+    )
     small_core_copy.start()
 
     def small_seq_copy(d):
@@ -396,39 +409,52 @@
             small_part, small_z.at[z], sc_s.at[d - 1], sc_r.at[d - 1], **at(2 * z_peer(d) + core, pos)
         )
 
+    def small_done_copy(which):
+        return pltpu.make_async_remote_copy(
+            small_all.at[which], small_all.at[which], sd_s, sd_r, **at(partner, pos)
+        )
+
+    to_z(0)
+
     small_core_copy.wait()
-    small_sum[...] = small[...] + small_core[...]
+    value = (small[core] + small_core[...]).astype(BF16)
+    small_sum[...] = value
+    small_seq[pos] = value
     for d in range(1, ns):
         small_seq_copy(d).start()
-    small_seq[pos] = small_sum[...]
-
-    to_z(0)
-
-    for d in range(1, ns):
-        small_seq_copy(d).wait()
-    total = small_seq[0]
-    for s in range(1, ns):
-        total = total + small_seq[s]
-    small_part[...] = total
-    for d in range(1, nz):
-        small_z_copy(d).start()
-    small_z[z] = total
 
     for q in range(1, PARTS + 2):
         if q < PARTS:
             to_z(q)
+        if q == max(PARTS - 1, 1):
+            for d in range(1, ns):
+                small_seq_copy(d).wait()
+            total = small_seq[0].astype(F32)
+            for p in range(1, ns):
+                total = total + small_seq[p].astype(F32)
+            value = total.astype(BF16)
+            small_part[...] = value
+            small_z[z] = value
+            for d in range(1, nz):
+                small_z_copy(d).start()
         if q - 1 < PARTS:
             finish_z(q - 1)
+        if q == PARTS:
+            for d in range(1, nz):
+                small_z_copy(d).wait()
+            total = small_z[0].astype(F32)
+            for p in range(1, nz):
+                total = total + small_z[p].astype(F32)
+            small_all[core] = total
+            small_done_copy(core).start()
         if q > 1:
             relay(q - 2)
 
-    for d in range(1, nz):
-        small_z_copy(d).wait()
-    total = small_z[0]
-    for s in range(1, nz):
-        total = total + small_z[s]
-    grad_one_out[...] = total[0:TAPS]
-    norms_out[...] = total[10:14]
+    small_done_copy(core).wait_send()
+    small_done_copy(1 - core).wait_recv()
+    for h in range(2):
+        grad_one_out[:, h * middle : (h + 1) * middle] = small_all[h, 0:TAPS]
+        norms_out[:, h * middle : (h + 1) * middle] = small_all[h, 10:14]
 
     for q in range(PARTS):
         for d in range(1, nz):
@@ -504,14 +530,15 @@
             pltpu.VMEM((PARTS, share, width), BF16),
             pltpu.VMEM((PARTS, nz - 1, piece, width), BF16),
             pltpu.VMEM((PARTS, 2, share, width), BF16),
-            pltpu.VMEM((16, channels), F32),
-            pltpu.VMEM((16, channels), F32),
-            pltpu.VMEM((16, channels), F32),
-            pltpu.VMEM((ns, 16, channels), F32),
-            pltpu.VMEM((16, channels), F32),
-            pltpu.VMEM((nz, 16, channels), F32),
+            pltpu.VMEM((2, 16, channels // 2), F32),
+            pltpu.VMEM((16, channels // 2), F32),
+            pltpu.VMEM((16, channels // 2), BF16),
+            pltpu.VMEM((ns, 16, channels // 2), BF16),
+            pltpu.VMEM((16, channels // 2), BF16),
+            pltpu.VMEM((nz, 16, channels // 2), BF16),
+            pltpu.VMEM((2, 16, channels // 2), F32),
             dma, dma,
-            dma((PARTS,)), dma((PARTS,)),
+            dma((PARTS, ns)), dma((PARTS, ns)),
             dma((PARTS, ns - 1)), dma((PARTS, ns - 1)),
             dma((PARTS, nz - 1)), dma((PARTS, nz - 1)),
             dma((PARTS, nz - 1)), dma((PARTS, nz - 1)),
@@ -519,6 +546,7 @@
             dma, dma,
             dma((ns - 1,)), dma((ns - 1,)),
             dma((nz - 1,)), dma((nz - 1,)),
+            dma, dma,
         ],
         compiler_params=pltpu.CompilerParams(
             collective_id=0, has_side_effects=True, vmem_limit_bytes=48 * 1024 * 1024

time: 43.5 us -> 37.8 us (0.87)
  Pallas kernels: 42.6 us -> 37 us
    pallas_call x1, Pallas kernels: 41.6 us -> 36 us  [on_device(): pl.pallas_call(functools.partial(kernel, ns, nz, pieces), out_shape=(jax....]
where the time goes in v3:
time: 37.8 us; the launch traced here: 37.6 us
  Pallas kernels  37 us (98%)
  between operations  0.64 us (2%)
    pallas_call x1, Pallas kernels, on_device(): pl.pallas_call(functools.partial(kernel, ns, nz, pieces), out_shape=(jax....  36 us
    pallas_call x1, Pallas kernels, on_device(): pl.pallas_call(put_out, out_shape=(jax.ShapeDtypeStruct((rows, channels),...  1.02 us

profile of v3, /device:TPU:0, one launch (start us, length us, event | category | flops | bytes accessed | tf_op | source)
XLA Modules:
  0.0 37.6 jit_solution(15805005706481608489)
XLA Ops:
  0.6 36.0 %shard_map.120 = (bf16[256,512]{1,0:T(8,128)(2,1)S(1)}, f32[10,512]{1,0:T(8,128)S(1)}, bf16[384,512]{1,0:T(8,128)(2,1)S(1)}, f32[4,512]{1,0:T(4,128)S(1)}) custom-call(bf16[4,640]{1,0:T(4,128)(2,1)} %wave_in.1, s32[1,4]{1,0:T(1,128)} %lengths_in.1, bf16[10,512]{1,0:T(8,128)(2,1)} %conv_one_in.1, bf16[1536,512]{1,0:T(8,128)(2,1)} %conv_two_in.1, ...), custom_call_target="tpu_custom_call" | custom-call | tf_op jit(solution)/shard_map/pallas_call | solution.py:491
  36.6 1.0 %shard_map.121 = (bf16[256,512]{1,0:T(8,128)(2,1)}, f32[10,512]{1,0:T(8,128)}, f32[384,512]{1,0:T(8,128)}, f32[4,512]{1,0:T(4,128)}) custom-call(bf16[256,512]{1,0:T(8,128)(2,1)S(1)} %get-tuple-element.12.features, f32[10,512]{1,0:T(8,128)S(1)} %get-tuple-element.13.grad_one, bf16[384,512]{1,0:T(8,128)(2,1)S(1)} %get-tuple-element.14.grad_two, ...), custom_call_target="tpu_custom_call" | custom-call | tf_op jit(solution)/shard_map/pallas_call | solution.py:568
